TPU v7x, 32 devices: a whole 2x2x4 slice. The times are simulated.
32 devices in a mesh: dp: 2 (over core), ctx: 4 (over y, x), tp: 4 (over z).
Axes of the slice: x: 2, y: 2, z: 4, core: 2. Of those that a mesh axis runs over, the one named last changes fastest.
Arguments:
- queries: bfloat16 [4, 8192, 1536], P('dp', 'tp', 'ctx'), may hold values from -6 to 6
- key_proj: bfloat16 [4, 8192, 1536], P('dp', 'tp', 'ctx'), may hold values from -6 to 6
- value_proj: bfloat16 [4, 8192, 1536], P('dp', 'tp', 'ctx'), may hold values from -6 to 6
- grad_output: bfloat16 [4, 8192, 1536], P('dp', 'tp', 'ctx'), may hold values from -6 to 6
- filters: float32 [512, 128], P('tp'), may hold values from -0.5 to 0.5
- group_of: int32 [8192], P('tp'), may hold values from 0 to 511, as said below
Outputs:
- gated_out: bfloat16 [4, 8192, 1536], P('dp', 'tp', 'ctx')
- grad_queries: bfloat16 [4, 8192, 1536], P('dp', 'tp', 'ctx')
- grad_keys: bfloat16 [4, 8192, 1536], P('dp', 'tp', 'ctx')
- grad_values: bfloat16 [4, 8192, 1536], P('dp', 'tp', 'ctx')
- grad_filters: float32 [512, 128], P('tp')
Inputs may be any that keep to these rules, and one draw needn't show every extreme that they name: `group_of`: channels come in aligned runs of 16 consecutive channels that share one filter row, and every filter row serves exactly one run.
All inputs are finite; a program needn't handle non-finite values.
Results may differ from a plain program's by a relative error of at most 0.0058.
Values may be sent and summed in bfloat16 or wider, within the bound.
No kernel may reach another device: no remote copies, remote signals or barrier semaphores. Data moves between devices by JAX's collectives and lax.ppermute only.
A program may use at most 192 MiB of HBM per device.

v0:
```python
import jax
import jax.numpy as jnp
from jax import lax
from jax.sharding import PartitionSpec as P

D = 8192
GROUPS = 512


def passed_along(block, axis, distance):
    devices = range(lax.axis_size(axis))
    route = [(i - distance, i) for i in devices if i - distance in devices]
    return lax.ppermute(block, axis, route)


def band_apply(matrix, rows_in, block_rows, groups_here):
    channels, positions = rows_in.shape
    blocked = rows_in.reshape(
        groups_here, channels // groups_here, positions // block_rows, block_rows
    )
    result = jnp.einsum("rmbj,rij->rmbi", blocked, matrix, preferred_element_type=jnp.float32)
    return result.reshape(channels, positions)


def band_adjoint(matrix, rows_in, block_rows, groups_here):
    channels, positions = rows_in.shape
    blocked = rows_in.reshape(
        groups_here, channels // groups_here, positions // block_rows, block_rows
    )
    result = jnp.einsum("rmbj,rji->rmbi", blocked, matrix, preferred_element_type=jnp.float32)
    return result.reshape(channels, positions)


def band_outer(left_rows, right_rows, block_rows, groups_here):
    channels, positions = left_rows.shape
    shape_four = (groups_here, channels // groups_here, positions // block_rows, block_rows)
    return jnp.einsum(
        "rmbi,rmbj->rij",
        left_rows.reshape(shape_four),
        right_rows.reshape(shape_four),
        preferred_element_type=jnp.float32,
    )


def shards(queries, key_proj, value_proj, grad_output, filters, group_of):
    wide = jnp.float32
    windows, channels, positions = queries.shape
    block_rows = filters.shape[1]
    members = D // GROUPS
    groups_here = channels // members
    filter_table = lax.all_gather(filters.astype(jnp.bfloat16), "tp", axis=0, tiled=True)
    run_group = group_of.reshape(groups_here, members)[:, 0]
    selector = (run_group[:, None] == jnp.arange(GROUPS, dtype=jnp.int32)[None, :]).astype(
        jnp.bfloat16
    )
    run_filters = jnp.dot(selector, filter_table, preferred_element_type=wide).astype(jnp.bfloat16)
    template = jnp.concatenate(
        [
            jnp.zeros((groups_here, 1), jnp.bfloat16),
            run_filters[:, ::-1],
            jnp.zeros((groups_here, block_rows), jnp.bfloat16),
        ],
        axis=1,
    )
    toeplitz = jnp.tile(template, (1, block_rows))[:, : 2 * block_rows * block_rows]
    toeplitz = toeplitz.reshape(groups_here, block_rows, 2 * block_rows)
    lower_band = toeplitz[:, :, :block_rows]
    upper_band = toeplitz[:, :, block_rows:]
    product = (key_proj.astype(wide) * value_proj.astype(wide)).astype(jnp.bfloat16)
    before = passed_along(product[:, :, -block_rows:], "ctx", 1)
    backward = (grad_output.astype(wide) * queries.astype(wide)).astype(jnp.bfloat16)
    after = passed_along(backward[:, :, :block_rows], "ctx", -1)
    gated_list = []
    gradq_list = []
    gradk_list = []
    gradv_list = []
    outer_total = jnp.zeros((groups_here, block_rows, 2 * block_rows), wide)
    for window in range(windows):
        product_w = product[window]
        backward_w = backward[window]
        previous = jnp.concatenate([before[window], product_w[:, :-block_rows]], axis=1)
        following = jnp.concatenate([backward_w[:, block_rows:], after[window]], axis=1)
        mixed_rows = band_apply(upper_band, product_w, block_rows, groups_here)
        mixed_rows = mixed_rows + band_apply(lower_band, previous, block_rows, groups_here)
        gated_list.append((queries[window].astype(wide) * mixed_rows).astype(jnp.bfloat16))
        gradq_list.append((grad_output[window].astype(wide) * mixed_rows).astype(jnp.bfloat16))
        upward = band_adjoint(upper_band, backward_w, block_rows, groups_here)
        upward = upward + band_adjoint(lower_band, following, block_rows, groups_here)
        gradk_list.append((upward * value_proj[window].astype(wide)).astype(jnp.bfloat16))
        gradv_list.append((upward * key_proj[window].astype(wide)).astype(jnp.bfloat16))
        outer_total = outer_total + jnp.concatenate(
            [
                band_outer(backward_w, previous, block_rows, groups_here),
                band_outer(backward_w, product_w, block_rows, groups_here),
            ],
            axis=2,
        )
    gated_out = jnp.stack(gated_list, axis=0)
    grad_queries = jnp.stack(gradq_list, axis=0)
    grad_keys = jnp.stack(gradk_list, axis=0)
    grad_values = jnp.stack(gradv_list, axis=0)
    flattened = outer_total.reshape(groups_here, 2 * block_rows * block_rows)
    flattened = jnp.pad(flattened, ((0, 0), (0, block_rows)))
    diagonals = jnp.sum(flattened.reshape(groups_here, block_rows, 2 * block_rows + 1), axis=1)
    run_grad = diagonals[:, block_rows:0:-1]
    scale_by = 1.0 / (windows * positions * lax.axis_size("dp") * lax.axis_size("ctx"))
    table_grad = (
        jnp.dot(selector.astype(wide).T, run_grad, precision=lax.Precision.HIGHEST) * scale_by
    )
    whole_grad = lax.psum(table_grad, ("dp", "ctx"))
    grad_filters = lax.psum_scatter(whole_grad, "tp", scatter_dimension=0, tiled=True)
    return (gated_out, grad_queries, grad_keys, grad_values, grad_filters)


def solution(mesh):
    in_specs = (
        P("dp", "tp", "ctx"),
        P("dp", "tp", "ctx"),
        P("dp", "tp", "ctx"),
        P("dp", "tp", "ctx"),
        P("tp", None),
        P("tp"),
    )
    out_specs = (
        P("dp", "tp", "ctx"),
        P("dp", "tp", "ctx"),
        P("dp", "tp", "ctx"),
        P("dp", "tp", "ctx"),
        P("tp", None),
    )
    return jax.shard_map(shards, mesh=mesh, in_specs=in_specs, out_specs=out_specs, check_vma=False)
```

profile of v0, /device:TPU:0, one launch (start us, length us, event | category | flops | bytes accessed | tf_op | source)
XLA Modules:
  0.0 380.6 jit_solution(17023830327281348778)
XLA Ops:
  7.2 3.8 multiply_convert_fusion
  11.0 1.1 slice.121
  12.0 1.3 collective-permute-start.1
  14.1 1.1 slice.112
  15.3 6.5 %collective-permute-start = (bf16[2,2048,128]{2,1,0:T(8,128)(2,1)}, bf16[2,2048,128]{2,1,0:T(8,128)(2,1)}, u32[]{:S(2)}, u32[]{:S(2)}) collective-permute-start(bf16[2,2048,128]{2,1,0:T(8,128)(2,1)} %slice.112), channel_id=1, source_target_pairs={{0,4},{4,8},{8,12},{1,5},{5,9},{9,13},{2,6},{6,10},{10,14},{3,7},{... | collective-permute-start | bytes 3145736 | tf_op jit(solution)/shard_map/ppermute | solution.py:13
  21.7 1.7 fusion.49
  23.5 1.0 slice.124
  24.8 14.4 %all_gather.3 = bf16[512,128]{1,0:T(8,128)(2,1)S(1)} all-gather(bf16[128,128]{1,0:T(8,128)(2,1)S(1)} %convert_element_type.96), channel_id=1, replica_groups=mesh['dp'=2,'ctx'=4,'tp'=4] {'tp'}, dimensions={0}, use_global_device_ids=true | all-gather | bytes 163840 | tf_op jit(solution)/shard_map/all_gather | solution.py:51
  39.8 4.5 %tile.4 = bf16[128,128,257]{0,2,1:T(8,128)(2,1)} broadcast(bf16[128,257]{0,1:T(8,128)(2,1)S(1)} %copy.57), dimensions={0,2} | broadcast | bytes 8487168 | tf_op jit(solution)/shard_map/tile | solution.py:65
  44.3 12.9 %tile.10 = bf16[128,32896]{0,1:T(8,128)(2,1)} reshape(bf16[128,128,257]{0,2,1:T(8,128)(2,1)} %tile.4) | data formatting | bytes 16842752 | tf_op jit(solution)/shard_map/tile | solution.py:65
  57.2 3.4 slice-done
  60.6 3.8 fusion.48
  64.4 6.7 %copy.88 = bf16[128,128,128]{2,1,0:T(8,128)(2,1)} copy(bf16[128,128,128]{0,2,1:T(8,128)(2,1)} %get-tuple-element.6) | data formatting | bytes 8388608
  71.1 2.0 reshape_squeeze.20
  73.1 6.7 %copy.87 = bf16[128,128,128]{2,1,0:T(8,128)(2,1)} copy(bf16[128,128,128]{0,2,1:T(8,128)(2,1)} %get-tuple-element.5) | data formatting | bytes 8388608
  79.9 3.9 %reshape_squeeze.21 = bf16[128,16,3,128]{3,2,1,0:T(4,128)(2,1)S(1)} reshape(bf16[1,2048,384]{2,1,0:T(8,128)(2,1)} %get-tuple-element.14) | data formatting | bytes 3145728 | tf_op jit(solution)/shard_map/reshape;squeeze | solution.py:27
  83.8 4.1 %fusion.50 = (bf16[1,2048,384]{2,1,0:T(8,128)(2,1)}, bf16[2048,384]{1,0:T(8,128)(2,1)S(1)}, bf16[2048,384]{1,0:T(8,128)(2,1)S(1)}, bf16[1,2048,384]{2,1,0:T(8,128)(2,1)}) fusion(bf16[2,2048,384]{2,1,0:T(8,128)(2,1)} %copy-done.6), kind=kLoop, calls=%fused_computation.77 | loop fusion | bytes 9437184 | tf_op jit(solution)/shard_map/slice | solution.py:79
  88.9 1.1 slice.118
  90.0 5.1 %reshape_squeeze.9 = bf16[128,16,3,128]{3,2,1,0:T(4,128)(2,1)} reshape(bf16[1,2048,384]{2,1,0:T(8,128)(2,1)} %get-tuple-element.22) | data formatting | bytes 3145728 | tf_op jit(solution)/shard_map/reshape;squeeze | solution.py:18
  95.1 5.2 %reshape_squeeze.8 = bf16[128,16,3,128]{3,2,1,0:T(4,128)(2,1)} reshape(bf16[1,2048,384]{2,1,0:T(8,128)(2,1)} %get-tuple-element.19) | data formatting | bytes 3145728 | tf_op jit(solution)/shard_map/reshape;squeeze | solution.py:18
  100.3 6.3 %convolution_bitcast_fusion = f32[128,128,128]{1,2,0:T(8,128)} fusion(bf16[128,16,3,128]{3,2,1,0:T(4,128)(2,1)} %reshape_squeeze.9, bf16[128,16,3,128]{3,2,1,0:T(4,128)(2,1)S(1)} %reshape_squeeze.21), kind=kOutput, calls=%fused_computation.19 | convolution fusion | flops 201326592 | bytes 11534336 | tf_op jit(solution)/shard_map/rmbi,rmbj->rij/dot_general | solution.py:37
  106.6 4.6 %convolution_bitcast_fusion.2 = f32[128,128,128]{1,2,0:T(8,128)} fusion(bf16[128,16,3,128]{3,2,1,0:T(4,128)(2,1)S(1)} %copy-done.7, bf16[128,16,3,128]{3,2,1,0:T(4,128)(2,1)S(1)} %copy-done.3), kind=kOutput, calls=%fused_computation.21 | convolution fusion | flops 201326592 | bytes 11534336 | tf_op jit(solution)/shard_map/rmbi,rmbj->rij/dot_general | solution.py:37
  111.2 1.3 slice_bitcast_fusion.3
  112.5 2.1 pad_maximum_fusion.4
  114.6 5.1 %reshape.132 = bf16[128,16,3,128]{3,2,1,0:T(4,128)(2,1)} reshape(bf16[2048,384]{1,0:T(8,128)(2,1)} %get-tuple-element.28) | data formatting | bytes 3145728 | tf_op jit(solution)/shard_map/reshape | solution.py:18
  119.7 5.6 %reshape.131 = bf16[128,16,3,128]{3,2,1,0:T(4,128)(2,1)} reshape(bf16[2048,384]{1,0:T(8,128)(2,1)} %get-tuple-element.27) | data formatting | bytes 3145728 | tf_op jit(solution)/shard_map/reshape | solution.py:18
  125.4 6.3 %convolution_bitcast_fusion.1 = f32[128,128,128]{1,2,0:T(8,128)} fusion(bf16[128,16,3,128]{3,2,1,0:T(4,128)(2,1)} %reshape.132, bf16[128,16,3,128]{3,2,1,0:T(4,128)(2,1)S(1)} %reshape_squeeze.21), kind=kOutput, calls=%fused_computation.20 | convolution fusion | flops 201326592 | bytes 11534336 | tf_op jit(solution)/shard_map/rmbi,rmbj->rij/dot_general | solution.py:37
  131.7 4.7 %convolution_bitcast_fusion.3 = f32[128,128,128]{1,2,0:T(8,128)} fusion(bf16[128,16,3,128]{3,2,1,0:T(4,128)(2,1)S(1)} %copy-done.11, bf16[128,16,3,128]{3,2,1,0:T(4,128)(2,1)S(1)} %copy-done.4), kind=kOutput, calls=%fused_computation.22 | convolution fusion | flops 201326592 | bytes 11534336 | tf_op jit(solution)/shard_map/rmbi,rmbj->rij/dot_general | solution.py:37
  136.4 4.6 %fusion.4 = f32[128,16,3,128]{3,1,2,0:T(8,128)} fusion(bf16[128,128,128]{2,1,0:T(8,128)(2,1)S(1)} %copy-done.2, bf16[128,16,3,128]{3,2,1,0:T(4,128)(2,1)S(1)} %copy-done.10), kind=kOutput, calls=%fused_computation.7 | convolution fusion | flops 201326592 | bytes 8912896 | tf_op jit(solution)/shard_map/rmbj,rij->rmbi/dot_general | solution.py:21
  141.0 4.6 %fusion.6 = f32[128,16,3,128]{3,1,2,0:T(8,128)} fusion(bf16[128,128,128]{2,1,0:T(8,128)(2,1)S(1)} %copy-done.2, bf16[128,16,3,128]{3,2,1,0:T(4,128)(2,1)S(1)} %copy-done.11), kind=kOutput, calls=%fused_computation.9 | convolution fusion | flops 201326592 | bytes 8912896 | tf_op jit(solution)/shard_map/rmbj,rij->rmbi/dot_general | solution.py:21
  145.7 1.3 slice_bitcast_fusion.1
  147.0 2.0 pad_maximum_fusion.6
  149.0 5.1 %reshape.133 = bf16[128,16,3,128]{3,2,1,0:T(4,128)(2,1)} reshape(bf16[2048,384]{1,0:T(8,128)(2,1)} %get-tuple-element.29) | data formatting | bytes 3145728 | tf_op jit(solution)/shard_map/reshape | solution.py:27
  154.1 4.2 %fusion.2 = f32[128,16,3,128]{3,1,2,0:T(8,128)S(1)} fusion(bf16[128,128,128]{2,1,0:T(8,128)(2,1)} %copy.88, bf16[128,16,3,128]{3,2,1,0:T(4,128)(2,1)} %reshape.133), kind=kOutput, calls=%fused_computation.5 | convolution fusion | flops 201326592 | bytes 8912896 | tf_op jit(solution)/shard_map/rmbj,rji->rmbi/dot_general | solution.py:30
  158.8 1.3 fusion.22
  160.1 3.8 copy.67
  163.9 6.0 %add.74 = f32[1,2048,384]{2,1,0:T(8,128)} reshape(f32[128,16,3,128]{3,2,1,0:T(4,128)} %copy.67) | data formatting | bytes 6291456 | tf_op jit(solution)/shard_map/add | solution.py:88
  169.9 5.3 %reshape.134 = bf16[128,16,3,128]{3,2,1,0:T(4,128)(2,1)} reshape(bf16[2048,384]{1,0:T(8,128)(2,1)} %get-tuple-element.30) | data formatting | bytes 3145728 | tf_op jit(solution)/shard_map/reshape | solution.py:27
  175.2 4.2 %fusion = f32[128,16,3,128]{3,1,2,0:T(8,128)S(1)} fusion(bf16[128,128,128]{2,1,0:T(8,128)(2,1)} %copy.88, bf16[128,16,3,128]{3,2,1,0:T(4,128)(2,1)} %reshape.134), kind=kOutput, calls=%fused_computation.3 | convolution fusion | flops 201326592 | bytes 8912896 | tf_op jit(solution)/shard_map/rmbj,rji->rmbi/dot_general | solution.py:30
  179.4 1.3 fusion.25
  180.8 3.8 copy.70
  184.5 6.2 %add.76 = f32[1,2048,384]{2,1,0:T(8,128)} reshape(f32[128,16,3,128]{3,2,1,0:T(4,128)} %copy.70) | data formatting | bytes 6291456 | tf_op jit(solution)/shard_map/add | solution.py:88
  190.8 6.2 %fusion.19 = f32[128,16,3,128]{3,1,2,0:T(8,128)S(1)} fusion(f32[128,16,3,128]{3,1,2,0:T(8,128)} %fusion.4, bf16[128,128,128]{2,1,0:T(8,128)(2,1)} %copy.87, bf16[128,16,3,128]{3,2,1,0:T(4,128)(2,1)S(1)} %copy-done.9), kind=kOutput, calls=%fused_computation.36 | convolution fusion | flops 202113024 | bytes 12058624 | tf_op jit(solution)/shard_map/rmbj,rij->rmbi/dot_general | solution.py:21
  196.9 3.8 copy.64
  200.7 6.2 %add.72 = f32[1,2048,384]{2,1,0:T(8,128)} reshape(f32[128,16,3,128]{3,2,1,0:T(4,128)} %copy.64) | data formatting | bytes 6291456 | tf_op jit(solution)/shard_map/add | solution.py:84
  206.9 6.2 %fusion.16 = f32[128,16,3,128]{3,1,2,0:T(8,128)S(1)} fusion(f32[128,16,3,128]{3,1,2,0:T(8,128)} %fusion.6, bf16[128,128,128]{2,1,0:T(8,128)(2,1)} %copy.87, bf16[128,16,3,128]{3,2,1,0:T(4,128)(2,1)S(1)} %copy-done.8), kind=kOutput, calls=%fused_computation.35 | convolution fusion | flops 202113024 | bytes 12058624 | tf_op jit(solution)/shard_map/rmbj,rij->rmbi/dot_general | solution.py:21
  213.1 3.7 copy.61
  216.8 6.2 %add.70 = f32[1,2048,384]{2,1,0:T(8,128)} reshape(f32[128,16,3,128]{3,2,1,0:T(4,128)} %copy.61) | data formatting | bytes 6291456 | tf_op jit(solution)/shard_map/add | solution.py:84
  223.0 17.8 %maximum_add_fusion = f32[128,128,256]{1,2,0:T(8,128)} fusion(f32[128,128,128]{1,2,0:T(8,128)} %convolution_bitcast_fusion.2, f32[128,128,128]{1,2,0:T(8,128)} %convolution_bitcast_fusion.3, f32[128,128,128]{1,2,0:T(8,128)} %convolution_bitcast_fusion, f32[128,128,128]{1,2,0:T(8,128)} %convolution_bitcast_fusion.1), kind=kLoop, calls=%fused_computation | loop fusion | flops 12582912 | bytes 50331648 | tf_op jit(solution)/shard_map/add | solution.py:91
  240.8 17.7 %copy.79 = f32[128,128,256]{0,2,1:T(8,128)} copy(f32[128,128,256]{1,2,0:T(8,128)} %maximum_add_fusion) | data formatting | bytes 33554432 | tf_op jit(solution)/shard_map/add | solution.py:91
  258.5 13.3 %pad.4 = f32[128,32896]{0,1:T(8,128)} pad(f32[128,32768]{0,1:T(8,128)} %bitcast.67, f32[]{:T(128)} %constant.4.clone.1), padding=0_0x0_128 | pad | bytes 33619972 | tf_op jit(solution)/shard_map/jit(_pad)/pad | solution.py:103
  271.8 17.5 %reshape.135 = f32[128,128,257]{0,2,1:T(8,128)} reshape(f32[128,32896]{0,1:T(8,128)} %pad.4) | data formatting | bytes 33685504 | tf_op jit(solution)/shard_map/reshape | solution.py:104
  289.2 6.9 %reduce_sum.9 = f32[128,257]{0,1:T(8,128)S(1)} reduce(f32[128,128,257]{0,2,1:T(8,128)} %reshape.135, f32[]{:T(128)} %constant.4.clone.1), dimensions={1}, to_apply=%region_0.1 | reduce | flops 4177792 | bytes 16974340 | tf_op jit(solution)/shard_map/reduce_sum | solution.py:104
  296.2 1.1 convolution_multiply_fusion
  297.4 4.5 %multiply_convert_fusion.3 = (bf16[1,2048,384]{2,1,0:T(8,128)(2,1)S(1)}, bf16[1,2048,384]{2,1,0:T(8,128)(2,1)S(1)}, bf16[1,2048,384]{2,1,0:T(8,128)(2,1)S(1)}, bf16[1,2048,384]{2,1,0:T(8,128)(2,1)S(1)}) fusion(f32[1,2048,384]{2,1,0:T(8,128)S(1)} %copy-done.12, bf16[2,2048,384]{2,1,0:T(8,128)(2,1)} %param.7, f32[1,2048,384]{2,1,0:T(8,128)} %add.76, ...), kind=kLoop, calls=%fused_computation.28 | loop fusion | flops 9437184 | bytes 18874368 | tf_op jit(solution)/shard_map/convert_element_type | solution.py:90
  301.9 2.0 pad_maximum_fusion.3
  303.9 1.3 copy-done.13
  306.1 1.5 multiply_convert_fusion.7
  307.6 2.0 pad_maximum_fusion.2
  309.6 2.0 pad_maximum_fusion.1
  311.6 5.9 %reduce-scatter.2.cloned.1.call-done = f32[128,128]{1,0:T(8,128)} async-done(((f32[512,128]{1,0:T(8,128)}), f32[128,128]{1,0:T(8,128)}) %reduce-scatter.2.cloned.1.call-update) | async-done | bytes 65552 | tf_op jit(solution)/shard_map/reduce_scatter | solution.py:111
  317.6 2.0 pad_maximum_fusion
  319.6 52.5 %all-reduce.3.cloned.1.call-done = f32[128,128]{1,0:T(8,128)} async-done(((f32[128,128]{1,0:T(8,128)}), f32[128,128]{1,0:T(8,128)}) %all-reduce.3.cloned.1.call-update) | async-done | bytes 65552 | tf_op jit(solution)/shard_map/psum | solution.py:110
  372.0 1.5 copy.122
  (69 shorter events, 4.3 us)
Async XLA Ops:
  7.2 310.4 %reduce-scatter.2.cloned.1.call-start = ((), (), s32[]{:S(2)}) async-start(), calls=%async_computation.1 | async-start | bytes 327680 | tf_op jit(solution)/shard_map/reduce_scatter | solution.py:111
  7.2 6.1 %copy-start.15 = (bf16[2,2048,384]{2,1,0:T(8,128)(2,1)S(1)}, bf16[2,2048,384]{2,1,0:T(8,128)(2,1)}, u32[]{:S(2)}) copy-start(bf16[2,2048,384]{2,1,0:T(8,128)(2,1)} %param.8) | copy-start | bytes 9437188
  7.2 6.1 %copy-start.16 = (bf16[2,2048,384]{2,1,0:T(8,128)(2,1)S(1)}, bf16[2,2048,384]{2,1,0:T(8,128)(2,1)}, u32[]{:S(2)}) copy-start(bf16[2,2048,384]{2,1,0:T(8,128)(2,1)} %param.7) | copy-start | bytes 9437188
  12.0 133.6 %collective-permute-start.1 = (bf16[2,2048,128]{2,1,0:T(8,128)(2,1)}, bf16[2,2048,128]{2,1,0:T(8,128)(2,1)}, u32[]{:S(2)}, u32[]{:S(2)}) collective-permute-start(bf16[2,2048,128]{2,1,0:T(8,128)(2,1)} %slice.121), channel_id=1, source_target_pairs={{4,0},{8,4},{12,8},{5,1},{9,5},{13,9},{6,2},{10,6},{14,10},{7,3},{... | collective-permute-start | bytes 3145736 | tf_op jit(solution)/shard_map/ppermute | solution.py:13
  14.1 9.3 %copy-start.6 = (bf16[2,2048,384]{2,1,0:T(8,128)(2,1)}, bf16[2,2048,384]{2,1,0:T(8,128)(2,1)S(1)}, u32[]{:S(2)}) copy-start(bf16[2,2048,384]{2,1,0:T(8,128)(2,1)S(1)} %multiply_convert_fusion.1) | copy-start | bytes 9437188
  15.3 95.9 %collective-permute-start = (bf16[2,2048,128]{2,1,0:T(8,128)(2,1)}, bf16[2,2048,128]{2,1,0:T(8,128)(2,1)}, u32[]{:S(2)}, u32[]{:S(2)}) collective-permute-start(bf16[2,2048,128]{2,1,0:T(8,128)(2,1)} %slice.112), channel_id=1, source_target_pairs={{0,4},{4,8},{8,12},{1,5},{5,9},{9,13},{2,6},{6,10},{10,14},{3,7},{... | collective-permute-start | bytes 3145736 | tf_op jit(solution)/shard_map/ppermute | solution.py:13
  23.4 1.1 copy-start.23
  23.4 1.3 copy-start.22
  57.2 3.4 slice-start
  100.3 6.3 %copy-start.3 = (bf16[128,16,3,128]{3,2,1,0:T(4,128)(2,1)S(1)}, bf16[128,16,3,128]{3,2,1,0:T(4,128)(2,1)}, u32[]{:S(2)}) copy-start(bf16[128,16,3,128]{3,2,1,0:T(4,128)(2,1)} %reshape_squeeze.20) | copy-start | bytes 4718596
  100.3 6.3 %copy-start.7 = (bf16[128,16,3,128]{3,2,1,0:T(4,128)(2,1)S(1)}, bf16[128,16,3,128]{3,2,1,0:T(4,128)(2,1)}, u32[]{:S(2)}) copy-start(bf16[128,16,3,128]{3,2,1,0:T(4,128)(2,1)} %reshape_squeeze.8) | copy-start | bytes 4718596
  106.6 5.9 %copy-start.20 = (bf16[2048,256]{1,0:T(8,128)(2,1)S(1)}, bf16[2048,256]{1,0:T(8,128)(2,1)}, u32[]{:S(2)}) copy-start(bf16[2048,256]{1,0:T(8,128)(2,1)} %slice.114) | copy-start | bytes 3145732
  106.6 5.9 %copy-start.21 = (bf16[2048,256]{1,0:T(8,128)(2,1)S(1)}, bf16[2048,256]{1,0:T(8,128)(2,1)}, u32[]{:S(2)}) copy-start(bf16[2048,256]{1,0:T(8,128)(2,1)} %slice.118) | copy-start | bytes 3145732
  125.3 6.3 %copy-start.4 = (bf16[128,16,3,128]{3,2,1,0:T(4,128)(2,1)S(1)}, bf16[128,16,3,128]{3,2,1,0:T(4,128)(2,1)}, u32[]{:S(2)}) copy-start(bf16[128,16,3,128]{3,2,1,0:T(4,128)(2,1)} %reshape_squeeze.20) | copy-start | bytes 4718596
  125.4 6.3 %copy-start.11 = (bf16[128,16,3,128]{3,2,1,0:T(4,128)(2,1)S(1)}, bf16[128,16,3,128]{3,2,1,0:T(4,128)(2,1)}, u32[]{:S(2)}) copy-start(bf16[128,16,3,128]{3,2,1,0:T(4,128)(2,1)} %reshape.131) | copy-start | bytes 4718596
  131.6 4.8 %copy-start.2 = (bf16[128,128,128]{2,1,0:T(8,128)(2,1)S(1)}, bf16[128,128,128]{2,1,0:T(8,128)(2,1)}, u32[]{:S(2)}) copy-start(bf16[128,128,128]{2,1,0:T(8,128)(2,1)} %copy.88) | copy-start | bytes 12582916
  131.6 4.8 %copy-start.10 = (bf16[128,16,3,128]{3,2,1,0:T(4,128)(2,1)S(1)}, bf16[128,16,3,128]{3,2,1,0:T(4,128)(2,1)}, u32[]{:S(2)}) copy-start(bf16[128,16,3,128]{3,2,1,0:T(4,128)(2,1)} %reshape.132) | copy-start | bytes 4718596
  141.0 5.9 %copy-start.19 = (bf16[2048,256]{1,0:T(8,128)(2,1)S(1)}, bf16[2048,256]{1,0:T(8,128)(2,1)}, u32[]{:S(2)}) copy-start(bf16[2048,256]{1,0:T(8,128)(2,1)} %slice.124) | copy-start | bytes 3145732
  154.1 4.2 %copy-start = (bf16[128,128,128]{2,1,0:T(8,128)(2,1)S(1)}, bf16[128,128,128]{2,1,0:T(8,128)(2,1)}, u32[]{:S(2)}) copy-start(bf16[128,128,128]{2,1,0:T(8,128)(2,1)} %copy.87) | copy-start | bytes 12582916
  154.1 4.7 %copy-start.5 = (bf16[128,16,3,128]{3,2,1,0:T(4,128)(2,1)S(1)}, bf16[128,16,3,128]{3,2,1,0:T(4,128)(2,1)}, u32[]{:S(2)}) copy-start(bf16[128,16,3,128]{3,2,1,0:T(4,128)(2,1)} %reshape_squeeze.20) | copy-start | bytes 4718596
  175.2 4.2 %copy-start.1 = (bf16[128,128,128]{2,1,0:T(8,128)(2,1)S(1)}, bf16[128,128,128]{2,1,0:T(8,128)(2,1)}, u32[]{:S(2)}) copy-start(bf16[128,128,128]{2,1,0:T(8,128)(2,1)} %copy.87) | copy-start | bytes 12582916
  184.5 6.2 %copy-start.9 = (bf16[128,16,3,128]{3,2,1,0:T(4,128)(2,1)S(1)}, bf16[128,16,3,128]{3,2,1,0:T(4,128)(2,1)}, u32[]{:S(2)}) copy-start(bf16[128,16,3,128]{3,2,1,0:T(4,128)(2,1)} %reshape_squeeze.9) | copy-start | bytes 4718596
  200.7 6.2 %copy-start.8 = (bf16[128,16,3,128]{3,2,1,0:T(4,128)(2,1)S(1)}, bf16[128,16,3,128]{3,2,1,0:T(4,128)(2,1)}, u32[]{:S(2)}) copy-start(bf16[128,16,3,128]{3,2,1,0:T(4,128)(2,1)} %reshape_squeeze.8) | copy-start | bytes 4718596
  289.2 8.1 %copy-start.12 = (f32[1,2048,384]{2,1,0:T(8,128)S(1)}, f32[1,2048,384]{2,1,0:T(8,128)}, u32[]{:S(2)}) copy-start(f32[1,2048,384]{2,1,0:T(8,128)} %add.74) | copy-start | bytes 9437188
  297.3 74.8 %all-reduce.3.cloned.1.call-start = ((), (), s32[]{:S(2)}) async-start(), calls=%async_computation.2 | async-start | bytes 131072 | tf_op jit(solution)/shard_map/psum | solution.py:110
  297.3 6.5 %copy-start.17 = (bf16[2,2048,384]{2,1,0:T(8,128)(2,1)S(1)}, bf16[2,2048,384]{2,1,0:T(8,128)(2,1)}, u32[]{:S(2)}) copy-start(bf16[2,2048,384]{2,1,0:T(8,128)(2,1)} %param.9) | copy-start | bytes 9437188
  297.3 6.5 %copy-start.18 = (bf16[2,2048,384]{2,1,0:T(8,128)(2,1)S(1)}, bf16[2,2048,384]{2,1,0:T(8,128)(2,1)}, u32[]{:S(2)}) copy-start(bf16[2,2048,384]{2,1,0:T(8,128)(2,1)} %param.6) | copy-start | bytes 9437188
  301.8 3.4 copy-start.13
  301.9 4.3 %copy-start.14 = (f32[1,2048,384]{2,1,0:T(8,128)S(1)}, f32[1,2048,384]{2,1,0:T(8,128)}, u32[]{:S(2)}) copy-start(f32[1,2048,384]{2,1,0:T(8,128)} %add.70) | copy-start | bytes 9437188
Sparse Core Ops, SparseCore 0:
  297.4 20.1 reduce-scatter.1
  320.6 51.4 all-reduce.2
where the time goes:
time: 386 us; the launch traced here: 381 us
  local copies, waits for them, and re-layouts  182 us (47%)
  waiting for transfers between devices  58.4 us (15%)
  matrix products  55.8 us (14%)
  other arithmetic  47.4 us (12%)
  between operations  14.6 us (4%)
  blocking collectives  14.4 us (4%)
  starting transfers between devices  7.83 us (2%)
    psum x1, waiting for transfers between devices, shards(): whole_grad = lax.psum(table_grad, ('dp', 'ctx'))  52.5 us
    dot_general x4, matrix products, band_outer(): jnp.einsum('rmbi,rmbj->rij', left_rows.reshape(shape_four), right_rows.re...  21.9 us
    dot_general x4, matrix products, band_apply(): jnp.einsum('rmbj,rij->rmbi', blocked, matrix, preferred_element_type=jnp....  21.6 us
    add x4, local copies, waits for them, and re-layouts, shards(): mixed_rows + band_apply(lower_band, previous, block_rows, groups_here)  19.9 us
    add x4, local copies, waits for them, and re-layouts, shards(): upward + band_adjoint(lower_band, following, block_rows, groups_here)  19.8 us
    add x1, other arithmetic, shards(): outer_total + jnp.concatenate([band_outer(backward_w, previous, block_row...  17.8 us
    unnamed x51, local copies, waits for them, and re-layouts  17.8 us
    add x1, local copies, waits for them, and re-layouts, shards(): outer_total + jnp.concatenate([band_outer(backward_w, previous, block_row...  17.7 us
  transfers between devices with their start and end apart: 4, of which 2 were waited for; matrix products, arithmetic and copies ran while one was open for 32% of the time, Pallas kernels for 0%

commit v1 on v0

--- a/solution.py
+++ b/solution.py
@@ -107,7 +107,8 @@
     table_grad = (
         jnp.dot(selector.astype(wide).T, run_grad, precision=lax.Precision.HIGHEST) * scale_by
     )
-    whole_grad = lax.psum(table_grad, ("dp", "ctx"))
+    parts = lax.all_gather(table_grad, ("dp", "ctx"), axis=0, tiled=False)
+    whole_grad = parts.sum(axis=0)
     grad_filters = lax.psum_scatter(whole_grad, "tp", scatter_dimension=0, tiled=True)
     return (gated_out, grad_queries, grad_keys, grad_values, grad_filters)
 

time: 386 us -> 342 us (0.89)
  waiting for transfers between devices: 58.4 us -> 14.4 us
  matrix products: 55.8 us -> 49.8 us
  local copies, waits for them, and re-layouts: 182 us -> 186 us
    psum x1 -> x0, waiting for transfers between devices: 52.5 us -> none  [shards(): whole_grad = lax.psum(table_grad, ('dp', 'ctx'))]
    reduce_scatter x1, waiting for transfers between devices: 5.94 us -> 14.3 us  [shards(): lax.psum_scatter(whole_grad, 'tp', scatter_dimension=0, tiled=True)]
    add x1, other arithmetic: 17.8 us -> 13.9 us  [shards(): outer_total + jnp.concatenate([band_outer(backward_w, previous, block_row...]
    unnamed x51 -> x48, local copies, waits for them, and re-layouts: 17.8 us -> 18.1 us
  transfers between devices with their start and end apart: 4 -> 4, of which waited for: 2 -> 1; matrix products, arithmetic and copies ran while one was open for 32% -> 41% of each run, Pallas kernels for 0% -> 0%
where the time goes in v1:
time: 342 us; the launch traced here: 337 us
  local copies, waits for them, and re-layouts  186 us (54%)
  other arithmetic  50 us (15%)
  matrix products  49.8 us (15%)
  between operations  14.6 us (4%)
  blocking collectives  14.4 us (4%)
  waiting for transfers between devices  14.4 us (4%)
  starting transfers between devices  8.05 us (2%)
    dot_general x4, matrix products, band_outer(): jnp.einsum('rmbi,rmbj->rij', left_rows.reshape(shape_four), right_rows.re...  21.3 us
    add x4, local copies, waits for them, and re-layouts, shards(): mixed_rows + band_apply(lower_band, previous, block_rows, groups_here)  19.8 us
    add x4, local copies, waits for them, and re-layouts, shards(): upward + band_adjoint(lower_band, following, block_rows, groups_here)  19.5 us
    dot_general x4, matrix products, band_apply(): jnp.einsum('rmbj,rij->rmbi', blocked, matrix, preferred_element_type=jnp....  19.1 us
    unnamed x48, local copies, waits for them, and re-layouts  18.1 us
    add x1, local copies, waits for them, and re-layouts, shards(): outer_total + jnp.concatenate([band_outer(backward_w, previous, block_row...  17.7 us
    reshape x1, local copies, waits for them, and re-layouts, shards(): flattened.reshape(groups_here, block_rows, 2 * block_rows + 1)  17.5 us
    another operation x2, local copies, waits for them, and re-layouts, shards(): jnp.tile(template, (1, block_rows))[:, :2 * block_rows * block_rows]  17.4 us
  transfers between devices with their start and end apart: 4, of which 1 were waited for; matrix products, arithmetic and copies ran while one was open for 41% of the time, Pallas kernels for 0%

profile of v1, /device:TPU:0, one launch (start us, length us, event | category | flops | bytes accessed | tf_op | source)
XLA Modules:
  0.0 336.8 jit_solution(5719579797917263187)
XLA Ops:
  7.2 3.8 %multiply_convert_fusion = bf16[2,2048,384]{2,1,0:T(8,128)(2,1)S(1)} fusion(bf16[2,2048,384]{2,1,0:T(8,128)(2,1)} %param.6, bf16[2,2048,384]{2,1,0:T(8,128)(2,1)} %param.9), kind=kLoop, calls=%fused_computation.1 | loop fusion | flops 6291456 | bytes 9437184 | tf_op jit(solution)/shard_map/convert_element_type | solution.py:71
  12.0 1.3 collective-permute-start.1
  14.1 1.1 slice.112
  15.2 6.5 %collective-permute-start = (bf16[2,2048,128]{2,1,0:T(8,128)(2,1)}, bf16[2,2048,128]{2,1,0:T(8,128)(2,1)}, u32[]{:S(2)}, u32[]{:S(2)}) collective-permute-start(bf16[2,2048,128]{2,1,0:T(8,128)(2,1)} %slice.112), channel_id=1, source_target_pairs={{0,4},{4,8},{8,12},{1,5},{5,9},{9,13},{2,6},{6,10},{10,14},{3,7},{... | collective-permute-start | bytes 3145736 | tf_op jit(solution)/shard_map/ppermute | solution.py:13
  21.7 2.2 fusion.49
  24.0 1.1 slice.124
  25.3 14.4 %all_gather.9 = bf16[512,128]{1,0:T(8,128)(2,1)S(1)} all-gather(bf16[128,128]{1,0:T(8,128)(2,1)S(1)} %convert_element_type.96), channel_id=1, replica_groups=mesh['dp'=2,'ctx'=4,'tp'=4] {'tp'}, dimensions={0}, use_global_device_ids=true | all-gather | bytes 163840 | tf_op jit(solution)/shard_map/all_gather | solution.py:51
  40.3 4.5 %tile.4 = bf16[128,128,257]{0,2,1:T(8,128)(2,1)} broadcast(bf16[128,257]{0,1:T(8,128)(2,1)S(1)} %copy.57), dimensions={0,2} | broadcast | bytes 8487168 | tf_op jit(solution)/shard_map/tile | solution.py:65
  44.8 12.9 %tile.10 = bf16[128,32896]{0,1:T(8,128)(2,1)} reshape(bf16[128,128,257]{0,2,1:T(8,128)(2,1)} %tile.4) | data formatting | bytes 16842752 | tf_op jit(solution)/shard_map/tile | solution.py:65
  57.7 3.4 %slice-done = bf16[128,32768]{0,1:T(8,128)(2,1)S(1)} async-done(((bf16[128,32896]{0,1:T(8,128)(2,1)}), bf16[128,32768]{0,1:T(8,128)(2,1)S(1)}, s32[]{:S(2)}) %slice-start) | async-done | bytes 8388632 | tf_op jit(solution)/shard_map/slice | solution.py:65
  61.1 3.8 %fusion.48 = (bf16[128,128,128]{0,2,1:T(8,128)(2,1)}, bf16[128,128,128]{0,2,1:T(8,128)(2,1)}) fusion(bf16[128,128,256]{0,2,1:T(8,128)(2,1)S(1)} %bitcast.69), kind=kLoop, calls=%fused_computation.75 | loop fusion | bytes 16777216 | tf_op jit(solution)/shard_map/slice | solution.py:68
  64.9 6.8 %copy.88 = bf16[128,128,128]{2,1,0:T(8,128)(2,1)} copy(bf16[128,128,128]{0,2,1:T(8,128)(2,1)} %get-tuple-element.6) | data formatting | bytes 8388608
  71.7 3.9 %reshape_squeeze.20 = bf16[128,16,3,128]{3,2,1,0:T(4,128)(2,1)S(1)} reshape(bf16[1,2048,384]{2,1,0:T(8,128)(2,1)} %get-tuple-element.11) | data formatting | bytes 3145728 | tf_op jit(solution)/shard_map/reshape;squeeze | solution.py:27
  75.6 6.7 %copy.87 = bf16[128,128,128]{2,1,0:T(8,128)(2,1)} copy(bf16[128,128,128]{0,2,1:T(8,128)(2,1)} %get-tuple-element.5) | data formatting | bytes 8388608
  82.3 5.1 %reshape_squeeze.21 = bf16[128,16,3,128]{3,2,1,0:T(4,128)(2,1)} reshape(bf16[1,2048,384]{2,1,0:T(8,128)(2,1)} %get-tuple-element.14) | data formatting | bytes 3145728 | tf_op jit(solution)/shard_map/reshape;squeeze | solution.py:27
  87.4 4.1 %fusion.50 = (bf16[1,2048,384]{2,1,0:T(8,128)(2,1)}, bf16[2048,384]{1,0:T(8,128)(2,1)S(1)}, bf16[2048,384]{1,0:T(8,128)(2,1)S(1)}, bf16[1,2048,384]{2,1,0:T(8,128)(2,1)}) fusion(bf16[2,2048,384]{2,1,0:T(8,128)(2,1)} %copy-done.5), kind=kLoop, calls=%fused_computation.77 | loop fusion | bytes 9437184 | tf_op jit(solution)/shard_map/slice | solution.py:79
  91.5 1.1 slice.114
  92.6 1.0 slice.118
  93.6 5.1 %reshape_squeeze.9 = bf16[128,16,3,128]{3,2,1,0:T(4,128)(2,1)} reshape(bf16[1,2048,384]{2,1,0:T(8,128)(2,1)} %get-tuple-element.22) | data formatting | bytes 3145728 | tf_op jit(solution)/shard_map/reshape;squeeze | solution.py:18
  98.8 5.1 %reshape_squeeze.8 = bf16[128,16,3,128]{3,2,1,0:T(4,128)(2,1)} reshape(bf16[1,2048,384]{2,1,0:T(8,128)(2,1)} %get-tuple-element.19) | data formatting | bytes 3145728 | tf_op jit(solution)/shard_map/reshape;squeeze | solution.py:18
  103.9 6.9 %convolution_bitcast_fusion = f32[128,128,128]{1,2,0:T(8,128)} fusion(bf16[128,16,3,128]{3,2,1,0:T(4,128)(2,1)} %reshape_squeeze.9, bf16[128,16,3,128]{3,2,1,0:T(4,128)(2,1)} %reshape_squeeze.21), kind=kOutput, calls=%fused_computation.19 | convolution fusion | flops 201326592 | bytes 11534336 | tf_op jit(solution)/shard_map/rmbi,rmbj->rij/dot_general | solution.py:37
  110.8 4.6 %convolution_bitcast_fusion.2 = f32[128,128,128]{1,2,0:T(8,128)} fusion(bf16[128,16,3,128]{3,2,1,0:T(4,128)(2,1)S(1)} %copy-done.6, bf16[128,16,3,128]{3,2,1,0:T(4,128)(2,1)S(1)} %reshape_squeeze.20), kind=kOutput, calls=%fused_computation.21 | convolution fusion | flops 201326592 | bytes 11534336 | tf_op jit(solution)/shard_map/rmbi,rmbj->rij/dot_general | solution.py:37
  115.4 1.3 slice_bitcast_fusion.1
  116.7 2.0 pad_maximum_fusion.6
  118.6 5.2 %reshape.133 = bf16[128,16,3,128]{3,2,1,0:T(4,128)(2,1)} reshape(bf16[2048,384]{1,0:T(8,128)(2,1)} %get-tuple-element.29) | data formatting | bytes 3145728 | tf_op jit(solution)/shard_map/reshape | solution.py:27
  123.9 1.3 slice_bitcast_fusion.3
  125.1 3.3 pad_maximum_fusion.4
  128.4 5.6 %reshape.132 = bf16[128,16,3,128]{3,2,1,0:T(4,128)(2,1)} reshape(bf16[2048,384]{1,0:T(8,128)(2,1)} %get-tuple-element.28) | data formatting | bytes 3145728 | tf_op jit(solution)/shard_map/reshape | solution.py:18
  134.1 6.9 %convolution_bitcast_fusion.1 = f32[128,128,128]{1,2,0:T(8,128)} fusion(bf16[128,16,3,128]{3,2,1,0:T(4,128)(2,1)} %reshape.132, bf16[128,16,3,128]{3,2,1,0:T(4,128)(2,1)} %reshape_squeeze.21), kind=kOutput, calls=%fused_computation.20 | convolution fusion | flops 201326592 | bytes 11534336 | tf_op jit(solution)/shard_map/rmbi,rmbj->rij/dot_general | solution.py:37
  141.0 4.7 %fusion.4 = f32[128,16,3,128]{3,1,2,0:T(8,128)} fusion(bf16[128,128,128]{2,1,0:T(8,128)(2,1)S(1)} %copy-done.3, bf16[128,16,3,128]{3,2,1,0:T(4,128)(2,1)S(1)} %copy-done.10), kind=kOutput, calls=%fused_computation.7 | convolution fusion | flops 201326592 | bytes 8912896 | tf_op jit(solution)/shard_map/rmbj,rij->rmbi/dot_general | solution.py:21
  145.7 1.2 fusion.2
  147.9 1.3 fusion.22
  149.2 3.7 %copy.67 = f32[128,16,3,128]{3,2,1,0:T(4,128)} copy(f32[128,16,3,128]{3,1,2,0:T(8,128)S(1)} %fusion.22) | data formatting | bytes 6291456 | tf_op jit(solution)/shard_map/add | solution.py:88
  152.9 6.0 %add.72 = f32[1,2048,384]{2,1,0:T(8,128)} reshape(f32[128,16,3,128]{3,2,1,0:T(4,128)} %copy.67) | data formatting | bytes 6291456 | tf_op jit(solution)/shard_map/add | solution.py:88
  158.9 5.3 %reshape.134 = bf16[128,16,3,128]{3,2,1,0:T(4,128)(2,1)} reshape(bf16[2048,384]{1,0:T(8,128)(2,1)} %get-tuple-element.30) | data formatting | bytes 3145728 | tf_op jit(solution)/shard_map/reshape | solution.py:27
  164.2 4.2 %fusion = f32[128,16,3,128]{3,1,2,0:T(8,128)S(1)} fusion(bf16[128,128,128]{2,1,0:T(8,128)(2,1)} %copy.88, bf16[128,16,3,128]{3,2,1,0:T(4,128)(2,1)} %reshape.134), kind=kOutput, calls=%fused_computation.3 | convolution fusion | flops 201326592 | bytes 8912896 | tf_op jit(solution)/shard_map/rmbj,rji->rmbi/dot_general | solution.py:30
  168.9 1.3 fusion.25
  170.2 3.7 %copy.70 = f32[128,16,3,128]{3,2,1,0:T(4,128)} copy(f32[128,16,3,128]{3,1,2,0:T(8,128)S(1)} %fusion.25) | data formatting | bytes 6291456 | tf_op jit(solution)/shard_map/add | solution.py:88
  174.0 6.0 %add.74 = f32[1,2048,384]{2,1,0:T(8,128)} reshape(f32[128,16,3,128]{3,2,1,0:T(4,128)} %copy.70) | data formatting | bytes 6291456 | tf_op jit(solution)/shard_map/add | solution.py:88
  180.0 5.1 %reshape.131 = bf16[128,16,3,128]{3,2,1,0:T(4,128)(2,1)} reshape(bf16[2048,384]{1,0:T(8,128)(2,1)} %get-tuple-element.27) | data formatting | bytes 3145728 | tf_op jit(solution)/shard_map/reshape | solution.py:18
  185.1 2.9 convolution_bitcast_fusion.3
  188.0 13.9 %maximum_add_fusion = f32[128,128,256]{1,2,0:T(8,128)} fusion(f32[128,128,128]{1,2,0:T(8,128)} %convolution_bitcast_fusion.2, f32[128,128,128]{1,2,0:T(8,128)S(1)} %convolution_bitcast_fusion.3, f32[128,128,128]{1,2,0:T(8,128)} %convolution_bitcast_fusion, f32[128,128,128]{1,2,0:T(8,128)} %convolution_bitcast_fusion.1), kind=kLoop, calls=%fused_computation | loop fusion | flops 12582912 | bytes 50331648 | tf_op jit(solution)/shard_map/add | solution.py:91
  201.9 17.7 %copy.79 = f32[128,128,256]{0,2,1:T(8,128)} copy(f32[128,128,256]{1,2,0:T(8,128)} %maximum_add_fusion) | data formatting | bytes 33554432 | tf_op jit(solution)/shard_map/add | solution.py:91
  219.6 13.3 %pad.4 = f32[128,32896]{0,1:T(8,128)} pad(f32[128,32768]{0,1:T(8,128)} %bitcast.68, f32[]{:T(128)} %constant.4.clone.1), padding=0_0x0_128 | pad | bytes 33619972 | tf_op jit(solution)/shard_map/jit(_pad)/pad | solution.py:103
  232.9 17.5 %reshape.135 = f32[128,128,257]{0,2,1:T(8,128)} reshape(f32[128,32896]{0,1:T(8,128)} %pad.4) | data formatting | bytes 33685504 | tf_op jit(solution)/shard_map/reshape | solution.py:104
  250.3 6.9 %reduce_sum.18 = f32[128,257]{0,1:T(8,128)S(1)} reduce(f32[128,128,257]{0,2,1:T(8,128)} %reshape.135, f32[]{:T(128)} %constant.4.clone.1), dimensions={1}, to_apply=%region_0.1 | reduce | flops 4177792 | bytes 16974340 | tf_op jit(solution)/shard_map/reduce_sum | solution.py:104
  257.3 1.1 convolution_multiply_fusion
  258.6 6.2 %fusion.19 = f32[128,16,3,128]{3,1,2,0:T(8,128)S(1)} fusion(f32[128,16,3,128]{3,1,2,0:T(8,128)} %fusion.4, bf16[128,128,128]{2,1,0:T(8,128)(2,1)} %copy.87, bf16[128,16,3,128]{3,2,1,0:T(4,128)(2,1)S(1)} %copy-done.8), kind=kOutput, calls=%fused_computation.36 | convolution fusion | flops 202113024 | bytes 12058624 | tf_op jit(solution)/shard_map/rmbj,rij->rmbi/dot_general | solution.py:21
  264.8 3.7 %copy.64 = f32[128,16,3,128]{3,2,1,0:T(4,128)} copy(f32[128,16,3,128]{3,1,2,0:T(8,128)S(1)} %fusion.19) | data formatting | bytes 6291456 | tf_op jit(solution)/shard_map/add | solution.py:84
  268.5 6.2 %add.70 = f32[1,2048,384]{2,1,0:T(8,128)} reshape(f32[128,16,3,128]{3,2,1,0:T(4,128)} %copy.64) | data formatting | bytes 6291456 | tf_op jit(solution)/shard_map/add | solution.py:84
  274.7 5.3 %fusion.6 = f32[128,16,3,128]{3,1,2,0:T(8,128)S(1)} fusion(bf16[128,128,128]{2,1,0:T(8,128)(2,1)} %copy.88, bf16[128,16,3,128]{3,2,1,0:T(4,128)(2,1)S(1)} %copy-done.9), kind=kOutput, calls=%fused_computation.9 | convolution fusion | flops 201326592 | bytes 8912896 | tf_op jit(solution)/shard_map/rmbj,rij->rmbi/dot_general | solution.py:21
  280.0 3.0 fusion.16
  283.0 3.7 %copy.61 = f32[128,16,3,128]{3,2,1,0:T(4,128)} copy(f32[128,16,3,128]{3,1,2,0:T(8,128)S(1)} %fusion.16) | data formatting | bytes 6291456 | tf_op jit(solution)/shard_map/add | solution.py:84
  286.8 6.2 %add.68 = f32[1,2048,384]{2,1,0:T(8,128)} reshape(f32[128,16,3,128]{3,2,1,0:T(4,128)} %copy.61) | data formatting | bytes 6291456 | tf_op jit(solution)/shard_map/add | solution.py:84
  292.9 4.3 %multiply_convert_fusion.3 = (bf16[1,2048,384]{2,1,0:T(8,128)(2,1)S(1)}, bf16[1,2048,384]{2,1,0:T(8,128)(2,1)S(1)}, bf16[1,2048,384]{2,1,0:T(8,128)(2,1)S(1)}, bf16[1,2048,384]{2,1,0:T(8,128)(2,1)S(1)}) fusion(f32[1,2048,384]{2,1,0:T(8,128)S(1)} %copy-done.11, bf16[2,2048,384]{2,1,0:T(8,128)(2,1)} %param.7, f32[1,2048,384]{2,1,0:T(8,128)} %add.74, ...), kind=kLoop, calls=%fused_computation.28 | loop fusion | flops 9437184 | bytes 18874368 | tf_op jit(solution)/shard_map/convert_element_type | solution.py:90
  297.3 2.0 pad_maximum_fusion.3
  299.3 2.0 pad_maximum_fusion.2
  301.3 1.1 copy-done.17
  302.4 1.1 copy-done.12
  304.4 2.6 multiply_convert_fusion.7
  307.1 2.4 reduce_sum.19
  309.5 3.9 %pad_maximum_fusion.1 = bf16[2,2048,384]{2,1,0:T(8,128)(2,1)} fusion(bf16[1,2048,384]{2,1,0:T(8,128)(2,1)} %get-tuple-element.16, bf16[1,2048,384]{2,1,0:T(8,128)(2,1)} %get-tuple-element.15), kind=kLoop, calls=%fused_computation.24 | loop fusion | flops 1572864 | bytes 6291456 | tf_op jit(solution)/shard_map/stack | solution.py:99
  313.4 2.0 pad_maximum_fusion
  315.4 14.3 %reduce-scatter.2.cloned.1.call-done = f32[128,128]{1,0:T(8,128)} async-done(((f32[512,128]{1,0:T(8,128)}), f32[128,128]{1,0:T(8,128)}) %reduce-scatter.2.cloned.1.call-update) | async-done | bytes 65552 | tf_op jit(solution)/shard_map/reduce_scatter | solution.py:112
  (67 shorter events, 5.5 us)
Async XLA Ops:
  7.2 299.9 %all-gather.3.cloned.1.call-start = ((), (), s32[]{:S(2)}) async-start(), calls=%async_computation.2 | async-start | bytes 2359296 | tf_op jit(solution)/shard_map/all_gather | solution.py:110
  7.2 6.1 %copy-start.14 = (bf16[2,2048,384]{2,1,0:T(8,128)(2,1)S(1)}, bf16[2,2048,384]{2,1,0:T(8,128)(2,1)}, u32[]{:S(2)}) copy-start(bf16[2,2048,384]{2,1,0:T(8,128)(2,1)} %param.8) | copy-start | bytes 9437188
  7.2 6.1 %copy-start.15 = (bf16[2,2048,384]{2,1,0:T(8,128)(2,1)S(1)}, bf16[2,2048,384]{2,1,0:T(8,128)(2,1)}, u32[]{:S(2)}) copy-start(bf16[2,2048,384]{2,1,0:T(8,128)(2,1)} %param.7) | copy-start | bytes 9437188
  12.0 103.4 %collective-permute-start.1 = (bf16[2,2048,128]{2,1,0:T(8,128)(2,1)}, bf16[2,2048,128]{2,1,0:T(8,128)(2,1)}, u32[]{:S(2)}, u32[]{:S(2)}) collective-permute-start(bf16[2,2048,128]{2,1,0:T(8,128)(2,1)} %slice.121), channel_id=1, source_target_pairs={{4,0},{8,4},{12,8},{5,1},{9,5},{13,9},{6,2},{10,6},{14,10},{7,3},{... | collective-permute-start | bytes 3145736 | tf_op jit(solution)/shard_map/ppermute | solution.py:13
  14.1 9.8 %copy-start.5 = (bf16[2,2048,384]{2,1,0:T(8,128)(2,1)}, bf16[2,2048,384]{2,1,0:T(8,128)(2,1)S(1)}, u32[]{:S(2)}) copy-start(bf16[2,2048,384]{2,1,0:T(8,128)(2,1)S(1)} %multiply_convert_fusion.1) | copy-start | bytes 9437188
  15.2 108.6 %collective-permute-start = (bf16[2,2048,128]{2,1,0:T(8,128)(2,1)}, bf16[2,2048,128]{2,1,0:T(8,128)(2,1)}, u32[]{:S(2)}, u32[]{:S(2)}) collective-permute-start(bf16[2,2048,128]{2,1,0:T(8,128)(2,1)} %slice.112), channel_id=1, source_target_pairs={{0,4},{4,8},{8,12},{1,5},{5,9},{9,13},{2,6},{6,10},{10,14},{3,7},{... | collective-permute-start | bytes 3145736 | tf_op jit(solution)/shard_map/ppermute | solution.py:13
  23.9 1.1 copy-start.22
  23.9 1.3 copy-start.21
  57.7 3.4 %slice-start = ((bf16[128,32896]{0,1:T(8,128)(2,1)}), bf16[128,32768]{0,1:T(8,128)(2,1)S(1)}, s32[]{:S(2)}) async-start(bf16[128,32896]{0,1:T(8,128)(2,1)} %tile.10), calls=%async_computation.3 | async-start | bytes 16777216 | tf_op jit(solution)/shard_map/slice | solution.py:65
  103.9 6.9 %copy-start.6 = (bf16[128,16,3,128]{3,2,1,0:T(4,128)(2,1)S(1)}, bf16[128,16,3,128]{3,2,1,0:T(4,128)(2,1)}, u32[]{:S(2)}) copy-start(bf16[128,16,3,128]{3,2,1,0:T(4,128)(2,1)} %reshape_squeeze.8) | copy-start | bytes 4718596
  110.8 5.9 %copy-start.19 = (bf16[2048,256]{1,0:T(8,128)(2,1)S(1)}, bf16[2048,256]{1,0:T(8,128)(2,1)}, u32[]{:S(2)}) copy-start(bf16[2048,256]{1,0:T(8,128)(2,1)} %slice.124) | copy-start | bytes 3145732
  118.6 6.5 %copy-start.20 = (bf16[2048,256]{1,0:T(8,128)(2,1)S(1)}, bf16[2048,256]{1,0:T(8,128)(2,1)}, u32[]{:S(2)}) copy-start(bf16[2048,256]{1,0:T(8,128)(2,1)} %slice.114) | copy-start | bytes 3145732
  134.1 7.0 %copy-start.3 = (bf16[128,128,128]{2,1,0:T(8,128)(2,1)S(1)}, bf16[128,128,128]{2,1,0:T(8,128)(2,1)}, u32[]{:S(2)}) copy-start(bf16[128,128,128]{2,1,0:T(8,128)(2,1)} %copy.88) | copy-start | bytes 12582916
  134.1 7.0 %copy-start.10 = (bf16[128,16,3,128]{3,2,1,0:T(4,128)(2,1)S(1)}, bf16[128,16,3,128]{3,2,1,0:T(4,128)(2,1)}, u32[]{:S(2)}) copy-start(bf16[128,16,3,128]{3,2,1,0:T(4,128)(2,1)} %reshape.132) | copy-start | bytes 4718596
  141.0 4.7 %copy-start.18 = (bf16[128,16,3,128]{3,2,1,0:T(4,128)(2,1)S(1)}, bf16[128,16,3,128]{3,2,1,0:T(4,128)(2,1)}, u32[]{:S(2)}) copy-start(bf16[128,16,3,128]{3,2,1,0:T(4,128)(2,1)} %reshape.133) | copy-start | bytes 4718596
  145.7 2.2 copy-start
  164.2 4.2 %copy-start.1 = (bf16[128,128,128]{2,1,0:T(8,128)(2,1)S(1)}, bf16[128,128,128]{2,1,0:T(8,128)(2,1)}, u32[]{:S(2)}) copy-start(bf16[128,128,128]{2,1,0:T(8,128)(2,1)} %copy.87) | copy-start | bytes 12582916
  164.2 4.7 %copy-start.4 = (bf16[128,16,3,128]{3,2,1,0:T(4,128)(2,1)S(1)}, bf16[128,16,3,128]{3,2,1,0:T(4,128)(2,1)}, u32[]{:S(2)}) copy-start(bf16[128,16,3,128]{3,2,1,0:T(4,128)(2,1)} %reshape_squeeze.21) | copy-start | bytes 4718596
  250.3 8.3 %copy-start.8 = (bf16[128,16,3,128]{3,2,1,0:T(4,128)(2,1)S(1)}, bf16[128,16,3,128]{3,2,1,0:T(4,128)(2,1)}, u32[]{:S(2)}) copy-start(bf16[128,16,3,128]{3,2,1,0:T(4,128)(2,1)} %reshape_squeeze.9) | copy-start | bytes 4718596
  258.4 71.4 %reduce-scatter.2.cloned.1.call-start = ((), (), s32[]{:S(2)}) async-start(), calls=%async_computation.1 | async-start | bytes 327680 | tf_op jit(solution)/shard_map/reduce_scatter | solution.py:112
  268.5 6.2 %copy-start.9 = (bf16[128,16,3,128]{3,2,1,0:T(4,128)(2,1)S(1)}, bf16[128,16,3,128]{3,2,1,0:T(4,128)(2,1)}, u32[]{:S(2)}) copy-start(bf16[128,16,3,128]{3,2,1,0:T(4,128)(2,1)} %reshape.131) | copy-start | bytes 4718596
  274.7 5.3 %copy-start.2 = (bf16[128,128,128]{2,1,0:T(8,128)(2,1)S(1)}, bf16[128,128,128]{2,1,0:T(8,128)(2,1)}, u32[]{:S(2)}) copy-start(bf16[128,128,128]{2,1,0:T(8,128)(2,1)} %copy.87) | copy-start | bytes 12582916
  274.7 5.3 %copy-start.7 = (bf16[128,16,3,128]{3,2,1,0:T(4,128)(2,1)S(1)}, bf16[128,16,3,128]{3,2,1,0:T(4,128)(2,1)}, u32[]{:S(2)}) copy-start(bf16[128,16,3,128]{3,2,1,0:T(4,128)(2,1)} %reshape_squeeze.8) | copy-start | bytes 4718596
  286.8 6.2 %copy-start.11 = (f32[1,2048,384]{2,1,0:T(8,128)S(1)}, f32[1,2048,384]{2,1,0:T(8,128)}, u32[]{:S(2)}) copy-start(f32[1,2048,384]{2,1,0:T(8,128)} %add.72) | copy-start | bytes 9437188
  297.3 4.1 %copy-start.16 = (bf16[2,2048,384]{2,1,0:T(8,128)(2,1)S(1)}, bf16[2,2048,384]{2,1,0:T(8,128)(2,1)}, u32[]{:S(2)}) copy-start(bf16[2,2048,384]{2,1,0:T(8,128)(2,1)} %param.9) | copy-start | bytes 9437188
  297.3 5.1 %copy-start.17 = (bf16[2,2048,384]{2,1,0:T(8,128)(2,1)S(1)}, bf16[2,2048,384]{2,1,0:T(8,128)(2,1)}, u32[]{:S(2)}) copy-start(bf16[2,2048,384]{2,1,0:T(8,128)(2,1)} %param.6) | copy-start | bytes 9437188
  299.3 4.2 %copy-start.12 = (f32[1,2048,384]{2,1,0:T(8,128)S(1)}, f32[1,2048,384]{2,1,0:T(8,128)}, u32[]{:S(2)}) copy-start(f32[1,2048,384]{2,1,0:T(8,128)} %add.70) | copy-start | bytes 9437188
  299.3 5.1 %copy-start.13 = (f32[1,2048,384]{2,1,0:T(8,128)S(1)}, f32[1,2048,384]{2,1,0:T(8,128)}, u32[]{:S(2)}) copy-start(f32[1,2048,384]{2,1,0:T(8,128)} %add.68) | copy-start | bytes 9437188
Sparse Core Ops, SparseCore 0:
  258.5 27.8 all-gather.2
  309.6 20.0 reduce-scatter.1
